TPU v7x, 32 devices: a whole 2x2x4 slice. The times are simulated.
32 devices in a mesh: pb: 8 (over z, x), row: 4 (over y, core).
Axes of the slice: x: 2, y: 2, z: 4, core: 2. Of those that a mesh axis runs over, the one named last changes fastest.
Arguments:
- kernels: bfloat16 [8, 4096, 4096], P('pb', 'row'), may hold values from -6 to 6
- orbitals: bfloat16 [4096, 1024], P('pb'), may hold values from -0.75 to 0.75
- pairs: int32 [8, 4, 2], replicated, may hold values from 0 to 15
- k_slot: int32 [16], replicated, may hold values from 0 to 15, each once
- pair_count: int32 [8], replicated, may hold values from 1 to 4, as said below
Outputs:
- exchange_fields: float32 [4, 1024, 1024], P('row', 'pb')
Inputs may be any that keep to these rules, and one draw needn't show every extreme that they name: `k_slot`: every slot holds exactly one k-point. pairs p < pair_count[q] are live; some transfer vector has all 4 live.
All inputs are finite; a program needn't handle non-finite values.
Results may differ from a plain program's by a relative error of at most 0.0029.
Values may be sent and summed in bfloat16 or wider, within the bound.
A program may use at most 128 MiB of HBM per device.

v0:
```python
import jax
import jax.numpy as jnp
from jax import lax
from jax.sharding import PartitionSpec as P


def slot_lookup(k_ids, k_slot):
    positions = jnp.arange(k_slot.shape[0], dtype=jnp.int32)
    return jnp.sum(jnp.where(k_ids[..., None] == positions, k_slot, 0), axis=-1)


def pair_products(weight, orbital_basis, pair_index, orb_width, pair_total, row_start, row_count):
    orb_left = lax.dynamic_slice_in_dim(orbital_basis, pair_index * orb_width, orb_width, 1)
    orb_right = lax.dynamic_slice_in_dim(
        orbital_basis, (pair_total + pair_index) * orb_width, orb_width, 1
    )
    left_rows = lax.dynamic_slice_in_dim(orb_left, row_start, row_count, 0)
    right_rows = lax.dynamic_slice_in_dim(orb_right, row_start, row_count, 0)
    contract = (((1,), (1,)), ((), ()))
    right_gram = lax.dot_general(
        right_rows, orb_right, contract, preferred_element_type=jnp.float32
    )
    first_term = jnp.dot(
        (weight * right_gram).astype(jnp.bfloat16), orb_left, preferred_element_type=jnp.float32
    )
    left_gram = lax.dot_general(left_rows, orb_left, contract, preferred_element_type=jnp.float32)
    second_hadamard = (weight * left_gram).astype(jnp.bfloat16)
    second_term = lax.dot_general(
        second_hadamard, right_rows, (((0,), (0,)), ((), ())), preferred_element_type=jnp.float32
    )
    return (first_term, second_term)


def shards(kernels, orbitals, pairs, k_slot, pair_count):
    pb_count = lax.axis_size("pb")
    row_devices = lax.axis_size("row")
    here_row = lax.axis_index("row")
    weight = kernels[0]
    row_count = weight.shape[0]
    point_total = weight.shape[1]
    pair_total = pairs.shape[1]
    k_total = k_slot.shape[0]
    orb_width = orbitals.shape[1] // k_total
    local_points = orbitals.shape[0]
    local_orbs = orbitals.reshape(local_points, k_total, orb_width)
    wanted = jnp.concatenate(
        [slot_lookup(pairs[:, :, 0], k_slot), slot_lookup(pairs[:, :, 1], k_slot)], axis=1
    )
    slot_share = 2 * pair_total // row_devices
    my_slots = lax.dynamic_slice_in_dim(wanted, here_row * slot_share, slot_share, 1)
    picked = jnp.take(local_orbs, my_slots, axis=1).reshape(
        local_points, pb_count, slot_share * orb_width
    )
    arrived_orbs = lax.all_to_all(picked, "pb", split_axis=1, concat_axis=0, tiled=True)
    orbital_basis = lax.all_gather(
        arrived_orbs.reshape(point_total, slot_share * orb_width), "row", axis=1, tiled=True
    )
    row_start = here_row * row_count
    first_list = []
    second_list = []
    for pair_index in range(pair_total):
        first_term, second_term = pair_products(
            weight, orbital_basis, pair_index, orb_width, pair_total, row_start, row_count
        )
        first_list.append(first_term)
        second_list.append(second_term)
    first_block = jnp.concatenate(first_list, axis=1)
    second_block = jnp.concatenate(second_list, axis=1)
    second_whole = lax.psum(second_block, "row")
    second_rows = lax.dynamic_slice_in_dim(second_whole, row_start, row_count, 0)
    contrib = jnp.concatenate([first_block, second_rows], axis=1)
    arrived = lax.all_to_all(contrib, "pb", split_axis=0, concat_axis=1, tiled=True)
    point_share = row_count // pb_count
    arrived = arrived.reshape(point_share, pb_count * 2 * pair_total, orb_width)
    targets = jnp.concatenate([pairs[:, :, 0], pairs[:, :, 1]], axis=1)
    pair_ids = jnp.arange(pair_total, dtype=jnp.int32)
    live_half = pair_ids[None, :] < pair_count[:, None]
    live_mask = jnp.concatenate([live_half, live_half], axis=1)
    k_ids = jnp.arange(k_total, dtype=jnp.int32)
    onehot = jnp.where((targets[..., None] == k_ids) & live_mask[..., None], 1.0, 0.0).astype(
        jnp.float32
    )
    onehot = onehot.reshape(pb_count * 2 * pair_total, k_total)
    fields = jnp.einsum("msn,sk->mkn", arrived, onehot, precision=lax.Precision.HIGHEST)
    return fields.reshape(1, point_share, k_total * orb_width)


def solution(mesh):
    placed = (P("pb", "row", None), P("pb", None), P(), P(), P())
    return jax.shard_map(
        shards, mesh=mesh, in_specs=placed, out_specs=P("row", "pb", None), check_vma=False
    )
```

profile of v0, /device:TPU:0, one launch (start us, length us, event | category | flops | bytes accessed | tf_op | source)
XLA Modules:
  0.0 276.9 jit_solution(14889424699236633594)
XLA Ops:
  6.5 0.8 fusion.76
  7.3 0.9 select_reduce_fusion.1
  8.7 1.5 copy.20
  10.2 0.6 gather_fusion
  11.1 32.8 %all_to_all.31 = bf16[512,8,128]{0,2,1:T(8,128)(2,1)S(1)} all-to-all(bf16[512,8,128]{0,2,1:T(8,128)(2,1)S(1)} %broadcast_select_fusion), channel_id=1, replica_groups=mesh['pb'=8,'row'=4] {'pb'}, dimensions={1} | all-to-all | bytes 2097152 | tf_op jit(solution)/shard_map/all_to_all | solution.py:54
  43.9 1.3 copy.22
  45.3 34.1 %all-gather.2.cloned.1.call-done = bf16[4096,512]{1,0:T(8,128)(2,1)} async-done(((bf16[4096,128]{1,0:T(8,128)(2,1)}), bf16[4096,512]{1,0:T(8,128)(2,1)}) %all-gather.2.cloned.1.call-update) | async-done | bytes 4194320 | tf_op jit(solution)/shard_map/all_gather | solution.py:55
  79.4 5.8 %fusion.75 = (bf16[4096,64]{1,0:T(8,128)(2,1)}, bf16[4096,64]{1,0:T(8,128)(2,1)}, bf16[4096,64]{1,0:T(8,128)(2,1)S(1)}, bf16[4096,64]{1,0:T(8,128)(2,1)}, bf16[4...) fusion(bf16[4096,512]{1,0:T(8,128)(2,1)} %all-gather.2.cloned.1.c, ...), kind=kLoop, calls=%fused_computation.82 | loop fusion | bytes 8388608 | tf_op jit(solution)/shard_map/dynamic_slice | solution.py:13
  85.3 9.3 %fusion.11 = f32[4096,64]{0,1:T(8,128)} fusion(bf16[4096,64]{1,0:T(8,128)(2,1)} %get-tuple-element.9, bf16[1,1024,4096]{2,1,0:T(8,128)(2,1)} %param.5, s32[]{:T(128)S(6)} %select_n.42, bf16[4096,64]{1,0:T(8,128)(2,1)} %get-tuple-element.16), kind=kOutput, calls=%fused_computation.21 | convolution fusion | flops 1086324736 | bytes 11011072 | tf_op jit(solution)/shard_map/dot_general | solution.py:28
  94.5 8.6 %fusion.8 = f32[4096,64]{0,1:T(8,128)} fusion(bf16[4096,64]{1,0:T(8,128)(2,1)} %get-tuple-element.10, bf16[1,1024,4096]{2,1,0:T(8,128)(2,1)} %param.5, s32[]{:T(128)S(6)} %select_n.42, bf16[4096,64]{1,0:T(8,128)(2,1)S(1)} %get-tuple-element.11), kind=kOutput, calls=%fused_computation.18 | convolution fusion | flops 1086324736 | bytes 11011072 | tf_op jit(solution)/shard_map/dot_general | solution.py:28
  103.1 8.5 %fusion.9 = f32[4096,64]{0,1:T(8,128)} fusion(bf16[4096,64]{1,0:T(8,128)(2,1)} %get-tuple-element.12, bf16[1,1024,4096]{2,1,0:T(8,128)(2,1)} %param.5, s32[]{:T(128)S(6)} %select_n.42, bf16[4096,64]{1,0:T(8,128)(2,1)S(1)} %get-tuple-element.13), kind=kOutput, calls=%fused_computation.19 | convolution fusion | flops 1086324736 | bytes 11011072 | tf_op jit(solution)/shard_map/dot_general | solution.py:28
  111.7 8.8 %fusion.10 = f32[4096,64]{0,1:T(8,128)} fusion(bf16[4096,64]{1,0:T(8,128)(2,1)} %get-tuple-element.14, bf16[1,1024,4096]{2,1,0:T(8,128)(2,1)} %param.5, s32[]{:T(128)S(6)} %select_n.42, bf16[4096,64]{1,0:T(8,128)(2,1)S(1)} %get-tuple-element.15), kind=kOutput, calls=%fused_computation.20 | convolution fusion | flops 1086324736 | bytes 11011072 | tf_op jit(solution)/shard_map/dot_general | solution.py:28
  120.5 4.3 %pad_maximum_fusion = f32[4096,256]{0,1:T(8,128)} fusion(f32[4096,64]{0,1:T(8,128)} %fusion.8, f32[4096,64]{0,1:T(8,128)} %fusion.9, f32[4096,64]{0,1:T(8,128)} %fusion.10, f32[4096,64]{0,1:T(8,128)S(1)} %copy-done.2), kind=kLoop, calls=%fused_computation.17 | loop fusion | flops 3145728 | bytes 8388608 | tf_op jit(solution)/shard_map/concatenate | solution.py:68
  124.8 8.8 %fusion.21 = f32[1024,512]{0,1:T(8,128)S(1)} fusion(bf16[4096,64]{1,0:T(8,128)(2,1)} %get-tuple-element.16, bf16[1,1024,4096]{2,1,0:T(8,128)(2,1)} %param.5, s32[]{:T(128)S(6)} %select_n.42, bf16[4096,512]{1,0:T(8,128)(2,1)} %all-gather.2.cloned.1.call-done), kind=kOutput, calls=%fused_computation.30 | convolution fusion | flops 1086324736 | bytes 11010052 | tf_op jit(solution)/shard_map/dot_general | solution.py:23
  133.6 8.9 %fusion.22 = f32[1024,512]{0,1:T(8,128)S(1)} fusion(f32[1024,512]{0,1:T(8,128)S(1)} %fusion.21, bf16[4096,64]{1,0:T(8,128)(2,1)} %copy-done.1, bf16[1,1024,4096]{2,1,0:T(8,128)(2,1)} %param.5, s32[]{:T(128)S(6)} %select_n.42, bf16[4096,512]{1,0:T(8,128)(2,1)} %all-gather.2.cloned.1.call-done), kind=kOutput, calls=%fused_computation.31 | convolution fusion | flops 1086324736 | bytes 11010052 | tf_op jit(solution)/shard_map/dot_general | solution.py:23
  142.5 9.2 %fusion.23 = f32[1024,512]{0,1:T(8,128)S(1)} fusion(f32[1024,512]{0,1:T(8,128)S(1)} %fusion.22, bf16[4096,64]{1,0:T(8,128)(2,1)} %copy-done, bf16[1,1024,4096]{2,1,0:T(8,128)(2,1)} %param.5, s32[]{:T(128)S(6)} %select_n.42, bf16[4096,512]{1,0:T(8,128)(2,1)} %all-gather.2.cloned.1.call-done), kind=kOutput, calls=%fused_computation.32 | convolution fusion | flops 1086324736 | bytes 11010052 | tf_op jit(solution)/shard_map/dot_general | solution.py:23
  151.7 8.5 %fusion.24 = f32[1024,512]{0,1:T(8,128)S(1)} fusion(f32[1024,512]{0,1:T(8,128)S(1)} %fusion.23, bf16[4096,64]{1,0:T(8,128)(2,1)S(1)} %get-tuple-element.11, bf16[1,1024,4096]{2,1,0:T(8,128)(2,1)} %param.5, s32[]{:T(128)S(6)} %select_n.42, bf16[4096,512]{1,0:T(8,128)(2,1)} %all-gather.2.cloned.1.call-done), kind=kOutput, calls=%fused_computation.33 | convolution fusion | flops 1086324736 | bytes 11010052 | tf_op jit(solution)/shard_map/dot_general | solution.py:23
  160.2 50.3 %all-reduce.2.cloned.1.call-done = f32[4096,256]{0,1:T(8,128)} async-done(((f32[4096,256]{0,1:T(8,128)}), f32[4096,256]{0,1:T(8,128)}) %all-reduce.2.cloned.1.call-update) | async-done | bytes 4194320 | tf_op jit(solution)/shard_map/psum | solution.py:69
  210.5 1.3 dynamic-slice_dynamic-update-slice_fusion
  211.8 1.5 copy_bitcast_fusion
  213.3 5.5 %all-to-all-start.1 = ((f32[8,128,512]{1,2,0:T(8,128)}), f32[8,128,512]{1,2,0:T(8,128)S(1)}, u32[]{:S(2)}, u32[]{:S(2)}) async-start(f32[8,128,512]{1,2,0:T(8,128)} %copy_bitcast_fusion), calls=%async_computation.1 | async-start | bytes 4194304 | tf_op jit(solution)/shard_map/all_to_all | solution.py:72
  219.2 47.5 %all-to-all-done.1 = f32[8,128,512]{1,2,0:T(8,128)S(1)} async-done(((f32[8,128,512]{1,2,0:T(8,128)}), f32[8,128,512]{1,2,0:T(8,128)S(1)}, u32[]{:S(2)}, u32[]{:S(2)}) %all-to-all-start.1) | async-done | bytes 2097184 | tf_op jit(solution)/shard_map/all_to_all | solution.py:72
  266.7 2.2 fusion.18
  269.1 1.0 copy.26
  (28 shorter events, 1.3 us)
Async XLA Ops:
  6.5 72.9 %all-gather.2.cloned.1.call-start = ((), (), s32[]{:S(2)}) async-start(), calls=%async_computation.2 | async-start | bytes 5242880 | tf_op jit(solution)/shard_map/all_gather | solution.py:55
  45.2 165.2 %all-reduce.2.cloned.1.call-start = ((), (), s32[]{:S(2)}) async-start(), calls=%async_computation.3 | async-start | bytes 8388608 | tf_op jit(solution)/shard_map/psum | solution.py:69
  85.2 17.9 %copy-start = (bf16[4096,64]{1,0:T(8,128)(2,1)}, bf16[4096,64]{1,0:T(8,128)(2,1)S(1)}, u32[]{:S(2)}) copy-start(bf16[4096,64]{1,0:T(8,128)(2,1)S(1)} %get-tuple-element.13) | copy-start | bytes 1572868
  85.2 26.4 %copy-start.1 = (bf16[4096,64]{1,0:T(8,128)(2,1)}, bf16[4096,64]{1,0:T(8,128)(2,1)S(1)}, u32[]{:S(2)}) copy-start(bf16[4096,64]{1,0:T(8,128)(2,1)S(1)} %get-tuple-element.15) | copy-start | bytes 1572868
  111.7 8.8 %copy-start.2 = (f32[4096,64]{0,1:T(8,128)S(1)}, f32[4096,64]{0,1:T(8,128)}, u32[]{:S(2)}) copy-start(f32[4096,64]{0,1:T(8,128)} %fusion.11) | copy-start | bytes 3145732
  151.7 67.1 %copy-start.3 = (s32[8]{0:T(128)S(1)}, s32[8]{0:T(128)}, u32[]{:S(2)}) copy-start(s32[8]{0:T(128)} %param.9) | copy-start | bytes 100
  213.3 53.4 %all-to-all-start.1 = ((f32[8,128,512]{1,2,0:T(8,128)}), f32[8,128,512]{1,2,0:T(8,128)S(1)}, u32[]{:S(2)}, u32[]{:S(2)}) async-start(f32[8,128,512]{1,2,0:T(8,128)} %copy_bitcast_fusion), calls=%async_computation.1 | async-start | bytes 4194304 | tf_op jit(solution)/shard_map/all_to_all | solution.py:72
Sparse Core Ops, SparseCore 0:
  45.3 34.0 all-gather.1
  124.9 85.4 all-reduce.1
where the time goes:
time: 277 us
  waiting for transfers between devices  132 us (48%)
  matrix products  72.9 us (26%)
  blocking collectives  32.8 us (12%)
  local copies, waits for them, and re-layouts  14.6 us (5%)
  between operations  13.5 us (5%)
  other arithmetic  5.63 us (2%)
  starting transfers between devices  5.55 us (2%)
    psum x1, waiting for transfers between devices, shards(): second_whole = lax.psum(second_block, 'row')  50.3 us
    all_to_all x1, waiting for transfers between devices, shards(): lax.all_to_all(contrib, 'pb', split_axis=0, concat_axis=1, tiled=True)  47.5 us
    dot_general x4, matrix products, pair_products(): jnp.dot((weight * right_gram).astype(jnp.bfloat16), orb_left, preferred_e...  35.4 us
    dot_general x4, matrix products, pair_products(): lax.dot_general(second_hadamard, right_rows, (((0,), (0,)), ((), ())), pr...  35.2 us
    all_gather x1, waiting for transfers between devices, shards(): lax.all_gather(arrived_orbs.reshape(point_total, slot_share * orb_width),...  34.1 us
    all_to_all x1, blocking collectives, shards(): lax.all_to_all(picked, 'pb', split_axis=1, concat_axis=0, tiled=True)  32.8 us
    dynamic_slice x1, local copies, waits for them, and re-layouts, pair_products(): lax.dynamic_slice_in_dim(orbital_basis, pair_index * orb_width, orb_width...  5.82 us
  transfers between devices with their start and end apart: 3, of which 3 were waited for; matrix products, arithmetic and copies ran while one was open for 13% of the time, Pallas kernels for 0%

commit v1 on v0

--- a/solution.py
+++ b/solution.py
@@ -1,7 +1,40 @@
+import functools
 import jax
 import jax.numpy as jnp
 from jax import lax
 from jax.sharding import PartitionSpec as P
+
+
+def carry_heaps(block_in, d_out):
+    block_in = jnp.moveaxis(block_in, 0, d_out)
+    long_array = block_in.shape
+    return block_in.reshape(
+        *long_array[:d_out], long_array[d_out] * long_array[d_out + 1], *long_array[d_out + 2 :]
+    )
+
+
+def obtain_tails(sheet, device_axis):
+    n_parts = lax.axis_size(device_axis)
+    known = sheet[None]
+    for j in range(n_parts.bit_length() - 1):
+        x_next = 1 << j
+        oldest = range(n_parts)
+        new = map(lambda t: (t, t ^ x_next), oldest)
+        near = list(new)
+        work_now = lax.ppermute(known, device_axis, near)
+        even = jnp.stack([known, work_now])
+        high = lax.axis_index(device_axis)
+        met_up = high >> j & 1
+        known = jnp.where(met_up == 0, even, even[::-1]).reshape(-1, *sheet.shape)
+    return known
+
+
+def expand_tails_all(x_local, own_rows, at_axis):
+    everything = obtain_tails(x_local, own_rows)
+    return carry_heaps(everything, at_axis)
+
+
+end_bands_now = functools.partial(expand_tails_all, own_rows="row", at_axis=1)
 
 
 def slot_lookup(k_ids, k_slot):
@@ -52,9 +85,7 @@
         local_points, pb_count, slot_share * orb_width
     )
     arrived_orbs = lax.all_to_all(picked, "pb", split_axis=1, concat_axis=0, tiled=True)
-    orbital_basis = lax.all_gather(
-        arrived_orbs.reshape(point_total, slot_share * orb_width), "row", axis=1, tiled=True
-    )
+    orbital_basis = end_bands_now(arrived_orbs.reshape(point_total, slot_share * orb_width))
     row_start = here_row * row_count
     first_list = []
     second_list = []

time: 277 us -> 299 us (1.079)
  waiting for transfers between devices: 132 us -> 146 us
  matrix products: 72.9 us -> 66.9 us
  other arithmetic: 5.63 us -> 11.6 us
  local copies, waits for them, and re-layouts: 14.6 us -> 19.3 us
    ppermute x0 -> x2, waiting for transfers between devices: none -> 49.1 us  [obtain_tails(): work_now = lax.ppermute(known, device_axis, near)]
    all_gather x1 -> x0, waiting for transfers between devices: 34.1 us -> none  [shards(): lax.all_gather(arrived_orbs.reshape(point_total, slot_share * orb_width),...]
    reshape x0 -> x1, local copies, waits for them, and re-layouts: none -> 6.46 us  [obtain_tails(): known = jnp.where(met_up == 0, even, even[::-1]).reshape(-1, *sheet.shape)]
    dot_general x4, matrix products: 35.2 us -> 31 us  [pair_products(): lax.dot_general(second_hadamard, right_rows, (((0,), (0,)), ((), ())), pr...]
    another operation x0 -> x3, other arithmetic: none -> 4.05 us  [obtain_tails(): even = jnp.stack([known, work_now])]
  transfers between devices with their start and end apart: 3 -> 4, of which waited for: 3 -> 4; matrix products, arithmetic and copies ran while one was open for 13% -> 11% of each run, Pallas kernels for 0% -> 0%
where the time goes in v1:
time: 299 us; the launch traced here: 298 us
  waiting for transfers between devices  146 us (49%)
  matrix products  66.9 us (22%)
  blocking collectives  32.8 us (11%)
  local copies, waits for them, and re-layouts  19.3 us (6%)
  between operations  13.6 us (5%)
  other arithmetic  11.6 us (4%)
  starting transfers between devices  7.1 us (2%)
    psum x1, waiting for transfers between devices, shards(): second_whole = lax.psum(second_block, 'row')  49.8 us
    ppermute x2, waiting for transfers between devices, obtain_tails(): work_now = lax.ppermute(known, device_axis, near)  49.1 us
    all_to_all x1, waiting for transfers between devices, shards(): lax.all_to_all(contrib, 'pb', split_axis=0, concat_axis=1, tiled=True)  47.5 us
    dot_general x4, matrix products, pair_products(): jnp.dot((weight * right_gram).astype(jnp.bfloat16), orb_left, preferred_e...  33.7 us
    all_to_all x1, blocking collectives, shards(): lax.all_to_all(picked, 'pb', split_axis=1, concat_axis=0, tiled=True)  32.8 us
    dot_general x4, matrix products, pair_products(): lax.dot_general(second_hadamard, right_rows, (((0,), (0,)), ((), ())), pr...  31 us
    reshape x1, local copies, waits for them, and re-layouts, obtain_tails(): known = jnp.where(met_up == 0, even, even[::-1]).reshape(-1, *sheet.shape)  6.46 us
  transfers between devices with their start and end apart: 4, of which 4 were waited for; matrix products, arithmetic and copies ran while one was open for 11% of the time, Pallas kernels for 0%

profile of v1, /device:TPU:0, one launch (start us, length us, event | category | flops | bytes accessed | tf_op | source)
XLA Modules:
  0.0 297.9 jit_solution(9298992009451815168)
XLA Ops:
  6.5 1.5 copy.22
  11.1 32.8 %all_to_all.31 = bf16[512,8,128]{0,2,1:T(8,128)(2,1)S(1)} all-to-all(bf16[512,8,128]{0,2,1:T(8,128)(2,1)S(1)} %broadcast_select_fusion), channel_id=1, replica_groups=mesh['pb'=8,'row'=4] {'pb'}, dimensions={1} | all-to-all | bytes 2097152 | tf_op jit(solution)/shard_map/all_to_all | solution.py:87
  44.6 2.6 collective-permute-done
  47.5 1.9 fusion.19
  49.4 1.5 collective-permute-start.1
  50.9 46.5 %collective-permute-done.1 = bf16[2,4096,128]{2,1,0:T(8,128)(2,1)} collective-permute-done((bf16[2,4096,128]{2,1,0:T(8,128)(2,1)}, bf16[2,4096,128]{2,1,0:T(8,128)(2,1)}, u32[]{:S(2)}, u32[]{:S(2)}) %collective-permute-start.1) | collective-permute-done | bytes 2097184 | tf_op jit(solution)/shard_map/ppermute | solution.py:24
  97.4 2.0 pad_maximum_fusion
  99.3 2.8 reverse_select_fusion
  102.1 6.5 %copy.26 = bf16[4,4096,128]{1,2,0:T(8,128)(2,1)} copy(bf16[4,4096,128]{2,1,0:T(8,128)(2,1)} %bitcast.84) | data formatting | bytes 8388608 | tf_op jit(solution)/shard_map/reshape | solution.py:28
  108.6 3.7 %fusion.77 = (bf16[4096,64]{0,1:T(8,128)(2,1)}, bf16[4096,64]{0,1:T(8,128)(2,1)S(1)}, bf16[4096,64]{0,1:T(8,128)(2,1)S(1)}, bf16[4096,64]{0,1:T(8,128)(2,1)S(1)}...) fusion(bf16[4096,512]{0,1:T(8,128)(2,1)} %bitcast.79), kind=kLoop, calls=%fused_computation.88 | loop fusion | bytes 8388608 | tf_op jit(solution)/shard_map/dynamic_slice | solution.py:46
  112.2 7.5 %fusion.8 = f32[4096,64]{0,1:T(8,128)S(1)} fusion(bf16[4096,64]{0,1:T(8,128)(2,1)S(1)} %get-tuple-element.10, bf16[1,1024,4096]{2,1,0:T(8,128)(2,1)} %param.5, s32[]{:T(128)S(6)} %select_n.62, bf16[4096,64]{0,1:T(8,128)(2,1)S(1)} %get-tuple-element.11), kind=kOutput, calls=%fused_computation.21 | convolution fusion | flops 1086324736 | bytes 10224640 | tf_op jit(solution)/shard_map/dot_general | solution.py:61
  119.8 7.2 %fusion.9 = f32[4096,64]{0,1:T(8,128)S(1)} fusion(bf16[4096,64]{0,1:T(8,128)(2,1)S(1)} %get-tuple-element.12, bf16[1,1024,4096]{2,1,0:T(8,128)(2,1)} %param.5, s32[]{:T(128)S(6)} %select_n.62, bf16[4096,64]{0,1:T(8,128)(2,1)S(1)} %get-tuple-element.13), kind=kOutput, calls=%fused_computation.22 | convolution fusion | flops 1086324736 | bytes 10224640 | tf_op jit(solution)/shard_map/dot_general | solution.py:61
  127.0 7.5 %fusion.10 = f32[4096,64]{0,1:T(8,128)S(1)} fusion(bf16[4096,64]{0,1:T(8,128)(2,1)} %get-tuple-element.14, bf16[1,1024,4096]{2,1,0:T(8,128)(2,1)} %param.5, s32[]{:T(128)S(6)} %select_n.62, bf16[4096,64]{0,1:T(8,128)(2,1)} %get-tuple-element.15), kind=kOutput, calls=%fused_computation.23 | convolution fusion | flops 1086324736 | bytes 10224640 | tf_op jit(solution)/shard_map/dot_general | solution.py:61
  134.5 8.8 %fusion.11 = f32[4096,64]{0,1:T(8,128)} fusion(bf16[4096,64]{0,1:T(8,128)(2,1)} %get-tuple-element.9, bf16[1,1024,4096]{2,1,0:T(8,128)(2,1)} %param.5, s32[]{:T(128)S(6)} %select_n.62, bf16[4096,64]{0,1:T(8,128)(2,1)} %get-tuple-element.16), kind=kOutput, calls=%fused_computation.24 | convolution fusion | flops 1086324736 | bytes 10224640 | tf_op jit(solution)/shard_map/dot_general | solution.py:61
  143.3 3.5 %pad_maximum_fusion.1 = f32[4096,256]{0,1:T(8,128)} fusion(f32[4096,64]{0,1:T(8,128)S(1)} %fusion.8, f32[4096,64]{0,1:T(8,128)S(1)} %fusion.9, f32[4096,64]{0,1:T(8,128)S(1)} %fusion.10, f32[4096,64]{0,1:T(8,128)} %fusion.11), kind=kLoop, calls=%fused_computation.19 | loop fusion | flops 3145728 | bytes 8388608 | tf_op jit(solution)/shard_map/concatenate | solution.py:99
  147.8 8.4 %fusion.23 = f32[1024,512]{0,1:T(8,128)S(1)} fusion(bf16[4096,64]{0,1:T(8,128)(2,1)S(1)} %copy-done.5, bf16[1,1024,4096]{2,1,0:T(8,128)(2,1)} %param.5, s32[]{:T(128)S(6)} %select_n.62, bf16[4096,512]{0,1:T(8,128)(2,1)} %bitcast.80), kind=kOutput, calls=%fused_computation.36 | convolution fusion | flops 1086324736 | bytes 9830404 | tf_op jit(solution)/shard_map/dot_general | solution.py:56
  156.2 8.4 %fusion.24 = f32[1024,512]{0,1:T(8,128)S(1)} fusion(f32[1024,512]{0,1:T(8,128)S(1)} %fusion.23, bf16[4096,64]{0,1:T(8,128)(2,1)S(1)} %copy-done.4, bf16[1,1024,4096]{2,1,0:T(8,128)(2,1)} %param.5, s32[]{:T(128)S(6)} %select_n.62, bf16[4096,512]{0,1:T(8,128)(2,1)} %bitcast.81), kind=kOutput, calls=%fused_computation.37 | convolution fusion | flops 1086324736 | bytes 9830404 | tf_op jit(solution)/shard_map/dot_general | solution.py:56
  164.6 8.4 %fusion.25 = f32[1024,512]{0,1:T(8,128)S(1)} fusion(f32[1024,512]{0,1:T(8,128)S(1)} %fusion.24, bf16[4096,64]{0,1:T(8,128)(2,1)S(1)} %copy-done.3, bf16[1,1024,4096]{2,1,0:T(8,128)(2,1)} %param.5, s32[]{:T(128)S(6)} %select_n.62, bf16[4096,512]{0,1:T(8,128)(2,1)} %bitcast.82), kind=kOutput, calls=%fused_computation.38 | convolution fusion | flops 1086324736 | bytes 9830404 | tf_op jit(solution)/shard_map/dot_general | solution.py:56
  173.0 8.6 %fusion.26 = f32[1024,512]{0,1:T(8,128)S(1)} fusion(f32[1024,512]{0,1:T(8,128)S(1)} %fusion.25, bf16[4096,64]{0,1:T(8,128)(2,1)S(1)} %copy-done.1, bf16[1,1024,4096]{2,1,0:T(8,128)(2,1)} %param.5, s32[]{:T(128)S(6)} %select_n.62, bf16[4096,512]{0,1:T(8,128)(2,1)} %bitcast.83), kind=kOutput, calls=%fused_computation.39 | convolution fusion | flops 1086324736 | bytes 9830404 | tf_op jit(solution)/shard_map/dot_general | solution.py:56
  181.6 49.8 %all-reduce.2.cloned.1.call-done = f32[4096,256]{0,1:T(8,128)} async-done(((f32[4096,256]{0,1:T(8,128)}), f32[4096,256]{0,1:T(8,128)}) %all-reduce.2.cloned.1.call-update) | async-done | bytes 4194320 | tf_op jit(solution)/shard_map/psum | solution.py:100
  232.8 1.5 copy_bitcast_fusion
  234.2 5.5 %all-to-all-start.1 = ((f32[8,128,512]{1,2,0:T(8,128)}), f32[8,128,512]{1,2,0:T(8,128)S(1)}, u32[]{:S(2)}, u32[]{:S(2)}) async-start(f32[8,128,512]{1,2,0:T(8,128)} %copy_bitcast_fusion), calls=%async_computation.1 | async-start | bytes 4194304 | tf_op jit(solution)/shard_map/all_to_all | solution.py:103
  240.1 47.5 %all-to-all-done.1 = f32[8,128,512]{1,2,0:T(8,128)S(1)} async-done(((f32[8,128,512]{1,2,0:T(8,128)}), f32[8,128,512]{1,2,0:T(8,128)S(1)}, u32[]{:S(2)}, u32[]{:S(2)}) %all-to-all-start.1) | async-done | bytes 2097184 | tf_op jit(solution)/shard_map/all_to_all | solution.py:103
  287.7 2.2 fusion.20
  (40 shorter events, 7.8 us)
Async XLA Ops:
  6.5 224.9 %all-reduce.2.cloned.1.call-start = ((), (), s32[]{:S(2)}) async-start(), calls=%async_computation.2 | async-start | bytes 8388608 | tf_op jit(solution)/shard_map/psum | solution.py:100
  44.6 2.7 collective-permute-start
  49.4 48.0 %collective-permute-start.1 = (bf16[2,4096,128]{2,1,0:T(8,128)(2,1)}, bf16[2,4096,128]{2,1,0:T(8,128)(2,1)}, u32[]{:S(2)}, u32[]{:S(2)}) collective-permute-start(bf16[2,4096,128]{2,1,0:T(8,128)(2,1)} %get-tuple-element.18), channel_id=1, source_target_pairs={{0,2},{1,3},{2,0},{3,1},{4,6},{5,7},{6,4},{7,5},{8,10},{9,11},{10,... | collective-permute-start | bytes 6291464 | tf_op jit(solution)/shard_map/ppermute | solution.py:24
  112.2 7.6 %copy-start = (bf16[4096,64]{0,1:T(8,128)(2,1)}, bf16[4096,64]{0,1:T(8,128)(2,1)S(1)}, u32[]{:S(2)}) copy-start(bf16[4096,64]{0,1:T(8,128)(2,1)S(1)} %get-tuple-element.11) | copy-start | bytes 1572868
  112.2 7.6 %copy-start.2 = (bf16[4096,64]{0,1:T(8,128)(2,1)}, bf16[4096,64]{0,1:T(8,128)(2,1)S(1)}, u32[]{:S(2)}) copy-start(bf16[4096,64]{0,1:T(8,128)(2,1)S(1)} %get-tuple-element.13) | copy-start | bytes 1572868
  146.7 1.0 copy-start.5
  147.8 8.4 %copy-start.4 = (bf16[4096,64]{0,1:T(8,128)(2,1)S(1)}, bf16[4096,64]{0,1:T(8,128)(2,1)}, u32[]{:S(2)}) copy-start(bf16[4096,64]{0,1:T(8,128)(2,1)} %get-tuple-element.15) | copy-start | bytes 1572868
  156.2 8.4 %copy-start.3 = (bf16[4096,64]{0,1:T(8,128)(2,1)S(1)}, bf16[4096,64]{0,1:T(8,128)(2,1)}, u32[]{:S(2)}) copy-start(bf16[4096,64]{0,1:T(8,128)(2,1)} %copy-done.2) | copy-start | bytes 1572868
  164.6 8.4 %copy-start.1 = (bf16[4096,64]{0,1:T(8,128)(2,1)S(1)}, bf16[4096,64]{0,1:T(8,128)(2,1)}, u32[]{:S(2)}) copy-start(bf16[4096,64]{0,1:T(8,128)(2,1)} %copy-done) | copy-start | bytes 1572868
  232.7 7.2 %copy-start.6 = (s32[8]{0:T(128)S(1)}, s32[8]{0:T(128)}, u32[]{:S(2)}) copy-start(s32[8]{0:T(128)} %param.9) | copy-start | bytes 100
  234.2 53.4 %all-to-all-start.1 = ((f32[8,128,512]{1,2,0:T(8,128)}), f32[8,128,512]{1,2,0:T(8,128)S(1)}, u32[]{:S(2)}, u32[]{:S(2)}) async-start(f32[8,128,512]{1,2,0:T(8,128)} %copy_bitcast_fusion), calls=%async_computation.1 | async-start | bytes 4194304 | tf_op jit(solution)/shard_map/all_to_all | solution.py:103
Sparse Core Ops, SparseCore 0:
  146.9 84.5 all-reduce.1
